TPU v7x, 256 devices: a whole 4x4x8 slice. The times are simulated.
256 devices in a mesh: row: 8 (over x, core), col: 32 (over y, z).
Axes of the slice: x: 4, y: 4, z: 8, core: 2. Of those that a mesh axis runs over, the one named last changes fastest.
Arguments:
- response: float32 [18432, 18432], P('row', 'col'), may hold values from 0.002 to 0.02
- tile_map: int32 [288, 288], P('row', 'col'), may hold values 0 or 1
- band_offsets: int32 [288, 2], P('row'), may hold values from -48 to 48, as said below
- prior_spectra: float32 [512, 18432], P(None, 'col'), may hold values from 0.5 to 2
- boot_counts: int32 [512, 18432], P('col', 'row'), may hold values from 0 to 3
- spectrum: float32 [18432], P('row'), may hold values from 5 to 50
Outputs:
- covariance: float32 [18432, 18432], P('row', 'col')
- unfolded: float32 [512, 18432], P(None, 'col')
Inputs may be any that keep to these rules, and one draw needn't show every extreme that they name: `band_offsets`: column 0 is at most 0 and column 1 at least 0; some tile row reaches -48 and some reaches 48.
All inputs are finite; a program needn't handle non-finite values. No bound on the sum of `tile_map` on one device may be relied on, other than what follows from the above.
Results may differ from a plain program's by a relative error of at most 0.0003.
Values sent between devices are 32-bit elements; how exact they have to be, the bound alone decides.
A program may use at most 64 MiB of HBM per device.

v0:
```python
import jax
import jax.numpy as jnp
from jax import lax
from jax.sharding import Mesh
from jax.sharding import PartitionSpec as P

COL = ("col_0", "col_1")


def own_rows_2(subtotal, axes):
    for axis in axes:
        subtotal = lax.psum_scatter(subtotal, axis, scatter_dimension=0, tiled=True)
    return subtotal


def in_one(arrays, axis):
    ends = [0]
    for a in arrays:
        ends.append(ends[-1] + a.size)
    subtotal = lax.psum(jnp.concatenate([a.ravel() for a in arrays]), axis)
    return tuple((subtotal[b:e].reshape(a.shape) for a, b, e in zip(arrays, ends, ends[1:])))


def laid_out(pieces, dim):
    dims = list(pieces.shape[1:])
    dims[dim] *= pieces.shape[0]
    return jnp.moveaxis(pieces, 0, dim).reshape(dims)


def gather_in_order(array, axes, turns):
    pieces = array[None]
    for k in turns:
        pieces = lax.all_gather(pieces, axes[k], axis=0, tiled=True)
    block = [lax.axis_size(axes[k]) for k in reversed(turns)]
    pieces = pieces.reshape(*block, *array.shape)
    turned = sorted(range(len(turns)), key=lambda place: turns[len(turns) - 1 - place])
    return pieces.transpose(*turned, *range(len(turns), pieces.ndim)).reshape(-1, *array.shape)


def whole_of(array, axes, turns, dim):
    return laid_out(gather_in_order(array, axes, turns), dim)


def on_device(response, tile_map, band_offsets, prior_spectra, boot_counts, spectrum):
    row_place = lax.axis_index("row")
    col_place = lax.axis_index(COL)
    tiles_down, tiles_across = tile_map.shape
    tile_size = response.shape[0] // tiles_down
    measured = row_place * tiles_down + jnp.arange(tiles_down, dtype=jnp.int32)[:, None]
    truth = col_place * tiles_across + jnp.arange(tiles_across, dtype=jnp.int32)[None, :]
    inside = (truth >= measured + band_offsets[:, 0:1]) & (truth <= measured + band_offsets[:, 1:2])
    kept = (truth == measured) | inside & (tile_map == 1)
    expanded = jnp.repeat(jnp.repeat(kept, tile_size, 0), tile_size, 1)
    masked = jnp.where(expanded, response, jnp.zeros_like(response))
    replicas = prior_spectra.shape[0]
    measured_bins = masked.shape[0]
    folded = own_rows_2(
        jnp.dot(
            prior_spectra,
            masked.T,
            precision=lax.Precision.HIGHEST,
            preferred_element_type=jnp.float32,
        ),
        COL,
    )
    ratios = boot_counts.astype(jnp.float32) * spectrum[None, :] / folded
    fragment = lax.all_gather(ratios, COL, axis=0, tiled=True)
    partial_value = jnp.dot(
        fragment, masked, precision=lax.Precision.HIGHEST, preferred_element_type=jnp.float32
    )
    column_sums = jnp.sum(masked, axis=0)
    summed, efficiency = in_one((partial_value, column_sums), "row")
    unfolded = prior_spectra * summed / efficiency[None, :]
    centred = unfolded - jnp.mean(unfolded, axis=0)[None, :]
    regrouped = lax.all_to_all(centred, COL, split_axis=0, concat_axis=1, tiled=True)
    own_rows = lax.dynamic_slice_in_dim(regrouped, row_place * measured_bins, measured_bins, 1)
    covariance = jnp.dot(
        whole_of(own_rows, COL, (0, 1), 0).T,
        centred,
        precision=lax.Precision.HIGHEST,
        preferred_element_type=jnp.float32,
    )
    return (covariance / (replicas - 1), unfolded)


def solution(mesh):
    torus = Mesh(mesh.devices.reshape(mesh.shape["row"], 4, 8), ("row", "col_0", "col_1"))
    return jax.shard_map(
        on_device,
        mesh=torus,
        in_specs=(
            P("row", COL),
            P("row", COL),
            P("row", None),
            P(None, COL),
            P(COL, "row"),
            P("row"),
        ),
        out_specs=(P("row", COL), P(None, COL)),
        check_vma=False,
    )
```

profile of v0, /device:TPU:1, one launch (start us, length us, event | category | flops | bytes accessed | tf_op | source)
XLA Modules:
  0.0 435.8 jit_solution(6520451407332182556)
XLA Ops:
  7.2 0.0 copy-start
  7.2 0.0 reduce-scatter.5.cloned.1.call-start
  7.3 0.8 add_bitcast_fusion.1
  8.0 0.8 and_or_fusion
  8.8 0.1 broadcast_in_dim.8
  8.9 0.1 reshape.49
  9.1 0.3 broadcast_in_dim.18
  9.4 0.0 copy-done
  9.4 14.7 %convolution_bitcast_fusion = f32[512,2304]{0,1:T(8,128)} fusion(f32[512,576]{0,1:T(8,128)S(1)} %copy-done, pred[2304,576]{0,1:T(32,128)(4,1)S(1)} %bitcast.21, f32[2304,576]{0,1:T(8,128)} %param.6), kind=kOutput, calls=%fused_computation.1 | convolution fusion | flops 8155054080 | bytes 12533760 | tf_op jit(solution)/shard_map/dot_general | solution.py:58
  24.1 0.0 reduce-scatter.5.cloned.1.call-update
  24.2 0.0 copy-start.2
  24.2 0.0 copy-start.3
  24.2 0.0 reduce-scatter.7.cloned.1.call-start
  24.2 57.5 %reduce-scatter.5.cloned.1.call-done = f32[128,2304]{0,1:T(8,128)} async-done(((f32[512,2304]{0,1:T(8,128)}), f32[128,2304]{0,1:T(8,128)}) %reduce-scatter.5.cloned.1.call-update) | async-done | bytes 1179664 | tf_op jit(solution)/shard_map/reduce_scatter | solution.py:12
  81.7 2.7 copy.34
  84.4 0.0 reduce-scatter.7.cloned.1.call-update
  84.4 0.0 all-gather.4.cloned.1.call-start
  84.5 35.1 %reduce-scatter.7.cloned.1.call-done = f32[16,2304]{1,0:T(8,128)} async-done(((f32[128,2304]{1,0:T(8,128)}), f32[16,2304]{1,0:T(8,128)}) %reduce-scatter.7.cloned.1.call-update) | async-done | bytes 147472 | tf_op jit(solution)/shard_map/reduce_scatter | solution.py:12
  119.5 0.0 copy-done.2
  119.5 0.0 copy-done.3
  119.5 1.6 multiply_divide_fusion.1
  121.1 0.0 all-gather.4.cloned.1.call-update
  121.2 0.2 all-reduce.2.cloned.1.call-start
  121.4 3.3 fusion
  124.7 80.6 %all-gather.4.cloned.1.call-done = f32[512,2304]{1,0:T(8,128)} async-done(((f32[16,2304]{1,0:T(8,128)}), f32[512,2304]{1,0:T(8,128)}) %all-gather.4.cloned.1.call-update) | async-done | bytes 4718608 | tf_op jit(solution)/shard_map/all_gather | solution.py:67
  205.3 13.8 %fusion.1 = f32[512,576]{1,0:T(8,128)S(1)} fusion(f32[512,2304]{1,0:T(8,128)} %all-gather.4.cloned.1.call-done, pred[2304,576]{0,1:T(32,128)(4,1)S(1)} %bitcast.23, f32[2304,576]{0,1:T(8,128)} %param.6), kind=kOutput, calls=%fused_computation.4 | convolution fusion | flops 8155054080 | bytes 12533760 | tf_op jit(solution)/shard_map/dot_general | solution.py:68
  219.1 1.6 reshape.51
  220.7 2.5 pad_maximum_fusion
  223.1 0.0 all-reduce.2.cloned.1.call-update
  223.1 0.0 copy-done.1
  223.2 0.4 copy.29
  223.6 66.6 %all-reduce.2.cloned.1.call-done = f32[295488]{0:T(1024)} async-done(((f32[295488]{0:T(1024)}), f32[295488]{0:T(1024)}) %all-reduce.2.cloned.1.call-update) | async-done | bytes 1181968 | tf_op jit(solution)/shard_map/psum | solution.py:20
  290.2 1.3 slice-done
  291.5 1.4 reshape.52
  292.9 0.0 slice-done.1
  292.9 1.5 fusion.4
  294.4 1.2 broadcast_subtract_fusion
  295.6 9.3 %all-to-all-start = ((f32[32,16,576]{2,1,0:T(8,128)}), f32[32,16,576]{2,1,0:T(8,128)S(1)}, u32[]{:S(2)}, u32[]{:S(2)}) async-start(f32[32,16,576]{2,1,0:T(8,128)} %bitcast.4), calls=%async_computation.1 | async-start | bytes 2621440 | tf_op jit(solution)/shard_map/all_to_all | solution.py:75
  304.9 0.0 all-gather.6.cloned.1.call-start
  305.0 27.2 %all-to-all-done = f32[32,16,576]{2,1,0:T(8,128)S(1)} async-done(((f32[32,16,576]{2,1,0:T(8,128)}), f32[32,16,576]{2,1,0:T(8,128)S(1)}, u32[]{:S(2)}, u32[]{:S(2)}) %all-to-all-start) | async-done | bytes 1179680 | tf_op jit(solution)/shard_map/all_to_all | solution.py:75
  332.1 1.5 copy.30
  333.6 1.9 all_to_all.17
  335.5 11.0 %all-gather = f32[64,2304]{1,0:T(8,128)} all-gather(f32[16,2304]{1,0:T(8,128)S(1)} %constant_dynamic-slice_fusion), channel_id=2, replica_groups=mesh['row'=8,'col_0'=4,'col_1'=8] {'col_0'}, dimensions={0}, use_global_device_ids=true | all-gather | bytes 737280 | tf_op jit(solution)/shard_map/all_gather | solution.py:33
  346.5 0.0 all-gather.6.cloned.1.call-update
  346.5 1.4 copy.32
  347.9 66.0 %all-gather.6.cloned.1.call-done = f32[32,16,2304]{2,1,0:T(8,128)} async-done(((f32[4,16,2304]{2,1,0:T(8,128)}), f32[32,16,2304]{2,1,0:T(8,128)}) %all-gather.6.cloned.1.call-update) | async-done | bytes 4718608 | tf_op jit(solution)/shard_map/all_gather | solution.py:33
  414.0 2.7 copy.31
  416.7 12.6 %convolution_multiply_fusion = f32[2304,576]{0,1:T(8,128)} fusion(f32[512,2304]{1,0:T(8,128)S(1)} %bitcast.24, f32[512,576]{1,0:T(8,128)} %broadcast_subtract_fusion), kind=kOutput, calls=%fused_computation | convolution fusion | flops 8155054080 | bytes 11206656 | tf_op jit(solution)/shard_map/dot_general | solution.py:77
  (7 shorter events, 0.0 us)
Async XLA Ops:
  7.2 2.3 copy-start
  7.2 74.6 %reduce-scatter.5.cloned.1.call-start = ((), (), s32[]{:S(2)}) async-start(), calls=%async_computation.3 | async-start | bytes 5898240 | tf_op jit(solution)/shard_map/reduce_scatter | solution.py:12
  24.2 95.4 %copy-start.2 = (s32[16,2304]{1,0:T(8,128)S(1)}, s32[16,2304]{1,0:T(8,128)}, u32[]{:S(2)}) copy-start(s32[16,2304]{1,0:T(8,128)} %param.10) | copy-start | bytes 442372
  24.2 95.4 %copy-start.3 = (f32[2304]{0:T(1024)S(1)}, f32[2304]{0:T(1024)}, u32[]{:S(2)}) copy-start(f32[2304]{0:T(1024)} %param.11) | copy-start | bytes 27652
  24.2 95.3 %reduce-scatter.7.cloned.1.call-start = ((), (), s32[]{:S(2)}) async-start(), calls=%async_computation.7 | async-start | bytes 1327104 | tf_op jit(solution)/shard_map/reduce_scatter | solution.py:12
  84.4 120.8 %all-gather.4.cloned.1.call-start = ((), (), s32[]{:S(2)}) async-start(), calls=%async_computation.4 | async-start | bytes 4866048 | tf_op jit(solution)/shard_map/all_gather | solution.py:67
  121.2 169.0 %all-reduce.2.cloned.1.call-start = ((), (), s32[]{:S(2)}) async-start(), calls=%async_computation.5 | async-start | bytes 2367488 | tf_op jit(solution)/shard_map/psum | solution.py:20
  220.7 2.5 copy-start.1
  290.2 1.3 slice-start
  291.5 1.4 slice-start.1
  295.6 36.5 %all-to-all-start = ((f32[32,16,576]{2,1,0:T(8,128)}), f32[32,16,576]{2,1,0:T(8,128)S(1)}, u32[]{:S(2)}, u32[]{:S(2)}) async-start(f32[32,16,576]{2,1,0:T(8,128)} %bitcast.4), calls=%async_computation.1 | async-start | bytes 2621440 | tf_op jit(solution)/shard_map/all_to_all | solution.py:75
  304.9 109.1 %all-gather.6.cloned.1.call-start = ((), (), s32[]{:S(2)}) async-start(), calls=%async_computation.6 | async-start | bytes 5308416 | tf_op jit(solution)/shard_map/all_gather | solution.py:33
Sparse Core Ops, SparseCore 0:
  24.3 57.4 reduce-scatter.4
  84.9 34.6 reduce-scatter.6
  122.7 82.5 all-gather.3
  223.3 66.8 all-reduce.1
  346.7 67.2 all-gather.5
where the time goes:
time: 436 us
  waiting for transfers between devices  333 us (76%)
  matrix products  41.1 us (9%)
  local copies, waits for them, and re-layouts  15.4 us (4%)
  between operations  13.9 us (3%)
  other arithmetic  11.6 us (3%)
  blocking collectives  11 us (3%)
  starting transfers between devices  9.69 us (2%)
    reduce_scatter x2, waiting for transfers between devices, own_rows_2(): subtotal = lax.psum_scatter(subtotal, axis, scatter_dimension=0, tiled=True)  92.6 us
    all_gather x1, waiting for transfers between devices, on_device(): fragment = lax.all_gather(ratios, COL, axis=0, tiled=True)  80.6 us
    psum x1, waiting for transfers between devices, in_one(): subtotal = lax.psum(jnp.concatenate([a.ravel() for a in arrays]), axis)  66.6 us
    all_gather x1, waiting for transfers between devices, gather_in_order(): pieces = lax.all_gather(pieces, axes[k], axis=0, tiled=True)  66 us
    all_to_all x1, waiting for transfers between devices, on_device(): lax.all_to_all(centred, COL, split_axis=0, concat_axis=1, tiled=True)  27.2 us
    dot_general x1, matrix products, on_device(): jnp.dot(prior_spectra, masked.T, precision=lax.Precision.HIGHEST, preferr...  14.7 us
    dot_general x1, matrix products, on_device(): jnp.dot(fragment, masked, precision=lax.Precision.HIGHEST, preferred_elem...  13.8 us
    dot_general x1, matrix products, on_device(): jnp.dot(whole_of(own_rows, COL, (0, 1), 0).T, centred, precision=lax.Prec...  12.6 us
  transfers between devices with their start and end apart: 6, of which 6 were waited for; matrix products, arithmetic and copies ran while one was open for 1% of the time, Pallas kernels for 0%

commit v1 on v0

--- a/solution.py
+++ b/solution.py
@@ -5,6 +5,13 @@
 from jax.sharding import PartitionSpec as P
 
 COL = ("col_0", "col_1")
+
+
+def swapped_in(x, name, along):
+    peers = lax.axis_size(name)
+    blocks = jnp.stack([x for _ in range(peers)])
+    blocks = lax.all_to_all(blocks, name, split_axis=0, concat_axis=0)
+    return jnp.concatenate(blocks, axis=along)
 
 
 def own_rows_2(subtotal, axes):
@@ -30,7 +37,7 @@
 def gather_in_order(array, axes, turns):
     pieces = array[None]
     for k in turns:
-        pieces = lax.all_gather(pieces, axes[k], axis=0, tiled=True)
+        pieces = swapped_in(pieces, axes[k], 0)
     block = [lax.axis_size(axes[k]) for k in reversed(turns)]
     pieces = pieces.reshape(*block, *array.shape)
     turned = sorted(range(len(turns)), key=lambda place: turns[len(turns) - 1 - place])

time: 436 us -> 491 us (1.13)
  the two profiles are of different devices: /device:TPU:1 before, /device:TPU:6 now
where the time goes in v1:
time: 491 us
  waiting for transfers between devices  379 us (77%)
  matrix products  41.1 us (8%)
  local copies, waits for them, and re-layouts  18.2 us (4%)
  starting transfers between devices  16.2 us (3%)
  between operations  13.9 us (3%)
  other arithmetic  11.6 us (2%)
  blocking collectives  10.8 us (2%)
    all_to_all x1, waiting for transfers between devices, swapped_in(): blocks = lax.all_to_all(blocks, name, split_axis=0, concat_axis=0)  105 us
    reduce_scatter x2, waiting for transfers between devices, own_rows_2(): subtotal = lax.psum_scatter(subtotal, axis, scatter_dimension=0, tiled=True)  96.2 us
    all_gather x1, waiting for transfers between devices, on_device(): fragment = lax.all_gather(ratios, COL, axis=0, tiled=True)  79.8 us
    psum x1, waiting for transfers between devices, in_one(): subtotal = lax.psum(jnp.concatenate([a.ravel() for a in arrays]), axis)  62.9 us
    all_to_all x1, waiting for transfers between devices, on_device(): lax.all_to_all(centred, COL, split_axis=0, concat_axis=1, tiled=True)  34.7 us
    dot_general x1, matrix products, on_device(): jnp.dot(prior_spectra, masked.T, precision=lax.Precision.HIGHEST, preferr...  14.7 us
    dot_general x1, matrix products, on_device(): jnp.dot(fragment, masked, precision=lax.Precision.HIGHEST, preferred_elem...  13.8 us
    dot_general x1, matrix products, on_device(): jnp.dot(whole_of(own_rows, COL, (0, 1), 0).T, centred, precision=lax.Prec...  12.6 us
  transfers between devices with their start and end apart: 6, of which 6 were waited for; matrix products, arithmetic and copies ran while one was open for 1% of the time, Pallas kernels for 0%

profile of v1, /device:TPU:6, one launch (start us, length us, event | category | flops | bytes accessed | tf_op | source)
XLA Modules:
  0.0 490.6 jit_solution(2258369504108413627)
XLA Ops:
  7.2 0.0 copy-start
  7.2 0.0 reduce-scatter.5.cloned.1.call-start
  7.3 0.8 add_bitcast_fusion.1
  8.0 0.8 and_or_fusion
  8.8 0.1 broadcast_in_dim.6
  8.9 0.1 reshape.50
  9.1 0.3 broadcast_in_dim.7
  9.4 0.0 copy-done
  9.4 14.7 %convolution_bitcast_fusion = f32[512,2304]{0,1:T(8,128)} fusion(f32[512,576]{0,1:T(8,128)S(1)} %copy-done, pred[2304,576]{0,1:T(32,128)(4,1)S(1)} %bitcast.20, f32[2304,576]{0,1:T(8,128)} %param.6), kind=kOutput, calls=%fused_computation.1 | convolution fusion | flops 8155054080 | bytes 12533760 | tf_op jit(solution)/shard_map/dot_general | solution.py:65
  24.1 0.0 reduce-scatter.5.cloned.1.call-update
  24.2 0.0 copy-start.2
  24.2 0.0 copy-start.3
  24.2 0.0 reduce-scatter.7.cloned.1.call-start
  24.2 56.7 %reduce-scatter.5.cloned.1.call-done = f32[128,2304]{0,1:T(8,128)} async-done(((f32[512,2304]{0,1:T(8,128)}), f32[128,2304]{0,1:T(8,128)}) %reduce-scatter.5.cloned.1.call-update) | async-done | bytes 1179664 | tf_op jit(solution)/shard_map/reduce_scatter | solution.py:19
  80.9 2.7 copy.34
  83.6 0.0 reduce-scatter.7.cloned.1.call-update
  83.6 0.0 all-gather.2.cloned.1.call-start
  83.7 39.5 %reduce-scatter.7.cloned.1.call-done = f32[16,2304]{1,0:T(8,128)} async-done(((f32[128,2304]{1,0:T(8,128)}), f32[16,2304]{1,0:T(8,128)}) %reduce-scatter.7.cloned.1.call-update) | async-done | bytes 147472 | tf_op jit(solution)/shard_map/reduce_scatter | solution.py:19
  123.2 0.0 copy-done.2
  123.2 0.0 copy-done.3
  123.2 1.6 multiply_divide_fusion.1
  124.8 0.0 all-gather.2.cloned.1.call-update
  124.8 0.2 all-reduce.2.cloned.1.call-start
  125.1 3.3 fusion
  128.3 79.8 %all-gather.2.cloned.1.call-done = f32[512,2304]{1,0:T(8,128)} async-done(((f32[16,2304]{1,0:T(8,128)}), f32[512,2304]{1,0:T(8,128)}) %all-gather.2.cloned.1.call-update) | async-done | bytes 4718608 | tf_op jit(solution)/shard_map/all_gather | solution.py:74
  208.1 13.8 %fusion.1 = f32[512,576]{1,0:T(8,128)S(1)} fusion(f32[512,2304]{1,0:T(8,128)} %all-gather.2.cloned.1.call-done, pred[2304,576]{0,1:T(32,128)(4,1)S(1)} %bitcast.22, f32[2304,576]{0,1:T(8,128)} %param.6), kind=kOutput, calls=%fused_computation.4 | convolution fusion | flops 8155054080 | bytes 12533760 | tf_op jit(solution)/shard_map/dot_general | solution.py:75
  221.9 1.6 reshape.52
  223.5 2.5 pad_maximum_fusion
  226.0 0.0 all-reduce.2.cloned.1.call-update
  226.0 0.0 copy-done.1
  226.0 0.4 copy.29
  226.4 62.9 %all-reduce.2.cloned.1.call-done = f32[295488]{0:T(1024)} async-done(((f32[295488]{0:T(1024)}), f32[295488]{0:T(1024)}) %all-reduce.2.cloned.1.call-update) | async-done | bytes 1181968 | tf_op jit(solution)/shard_map/psum | solution.py:27
  289.3 1.3 slice-done
  290.6 1.4 reshape.53
  292.0 0.0 slice-done.1
  292.0 1.5 fusion.4
  293.5 1.2 broadcast_subtract_fusion
  294.7 9.9 %all-to-all-start = ((f32[32,16,576]{2,1,0:T(8,128)}), f32[32,16,576]{2,1,0:T(8,128)S(1)}, u32[]{:S(2)}, u32[]{:S(2)}) async-start(f32[32,16,576]{2,1,0:T(8,128)} %bitcast.4), calls=%async_computation.1 | async-start | bytes 2621440 | tf_op jit(solution)/shard_map/all_to_all | solution.py:82
  304.6 34.7 %all-to-all-done = f32[32,16,576]{2,1,0:T(8,128)S(1)} async-done(((f32[32,16,576]{2,1,0:T(8,128)}), f32[32,16,576]{2,1,0:T(8,128)S(1)}, u32[]{:S(2)}, u32[]{:S(2)}) %all-to-all-start) | async-done | bytes 1179680 | tf_op jit(solution)/shard_map/all_to_all | solution.py:82
  339.2 1.5 copy.30
  340.7 1.9 all_to_all.23
  342.7 10.8 %all_to_all.29 = f32[4,1,16,2304]{3,2,1,0:T(8,128)S(1)} all-to-all(f32[4,1,16,2304]{3,2,1,0:T(8,128)S(1)} %stack.6), channel_id=1, replica_groups=mesh['row'=8,'col_0'=4,'col_1'=8] {'col_0'}, dimensions={0} | all-to-all | bytes 1179648 | tf_op jit(solution)/shard_map/all_to_all | solution.py:13
  353.5 2.7 stack.7
  356.2 6.0 %all-to-all-start.2 = ((f32[8,4,16,2304]{3,2,1,0:T(8,128)}), f32[8,4,16,2304]{3,2,1,0:T(8,128)}, u32[]{:S(2)}, u32[]{:S(2)}) async-start(f32[8,4,16,2304]{3,2,1,0:T(8,128)} %stack.7), calls=%async_computation.3 | async-start | bytes 9437184 | tf_op jit(solution)/shard_map/all_to_all | solution.py:13
  362.2 1.4 copy.32
  363.6 105.2 %all-to-all-done.2 = f32[8,4,16,2304]{3,2,1,0:T(8,128)} async-done(((f32[8,4,16,2304]{3,2,1,0:T(8,128)}), f32[8,4,16,2304]{3,2,1,0:T(8,128)}, u32[]{:S(2)}, u32[]{:S(2)}) %all-to-all-start.2) | async-done | bytes 4718624 | tf_op jit(solution)/shard_map/all_to_all | solution.py:13
  468.8 2.7 copy.31
  471.5 12.6 %convolution_multiply_fusion = f32[2304,576]{0,1:T(8,128)} fusion(f32[512,2304]{1,0:T(8,128)S(1)} %bitcast.23, f32[512,576]{1,0:T(8,128)} %broadcast_subtract_fusion), kind=kOutput, calls=%fused_computation | convolution fusion | flops 8155054080 | bytes 11206656 | tf_op jit(solution)/shard_map/dot_general | solution.py:84
  (8 shorter events, 0.1 us)
Async XLA Ops:
  7.2 2.3 copy-start
  7.2 73.8 %reduce-scatter.5.cloned.1.call-start = ((), (), s32[]{:S(2)}) async-start(), calls=%async_computation.5 | async-start | bytes 5898240 | tf_op jit(solution)/shard_map/reduce_scatter | solution.py:19
  24.2 99.0 %copy-start.2 = (s32[16,2304]{1,0:T(8,128)S(1)}, s32[16,2304]{1,0:T(8,128)}, u32[]{:S(2)}) copy-start(s32[16,2304]{1,0:T(8,128)} %param.10) | copy-start | bytes 442372
  24.2 99.0 %copy-start.3 = (f32[2304]{0:T(1024)S(1)}, f32[2304]{0:T(1024)}, u32[]{:S(2)}) copy-start(f32[2304]{0:T(1024)} %param.11) | copy-start | bytes 27652
  24.2 99.0 %reduce-scatter.7.cloned.1.call-start = ((), (), s32[]{:S(2)}) async-start(), calls=%async_computation.8 | async-start | bytes 1327104 | tf_op jit(solution)/shard_map/reduce_scatter | solution.py:19
  83.6 124.5 %all-gather.2.cloned.1.call-start = ((), (), s32[]{:S(2)}) async-start(), calls=%async_computation.6 | async-start | bytes 4866048 | tf_op jit(solution)/shard_map/all_gather | solution.py:74
  124.8 164.5 %all-reduce.2.cloned.1.call-start = ((), (), s32[]{:S(2)}) async-start(), calls=%async_computation.7 | async-start | bytes 2367488 | tf_op jit(solution)/shard_map/psum | solution.py:27
  223.5 2.5 copy-start.1
  289.3 1.3 slice-start
  290.6 1.4 slice-start.1
  294.7 44.5 %all-to-all-start = ((f32[32,16,576]{2,1,0:T(8,128)}), f32[32,16,576]{2,1,0:T(8,128)S(1)}, u32[]{:S(2)}, u32[]{:S(2)}) async-start(f32[32,16,576]{2,1,0:T(8,128)} %bitcast.4), calls=%async_computation.1 | async-start | bytes 2621440 | tf_op jit(solution)/shard_map/all_to_all | solution.py:82
  356.2 112.6 %all-to-all-start.2 = ((f32[8,4,16,2304]{3,2,1,0:T(8,128)}), f32[8,4,16,2304]{3,2,1,0:T(8,128)}, u32[]{:S(2)}, u32[]{:S(2)}) async-start(f32[8,4,16,2304]{3,2,1,0:T(8,128)} %stack.7), calls=%async_computation.3 | async-start | bytes 9437184 | tf_op jit(solution)/shard_map/all_to_all | solution.py:13
Sparse Core Ops, SparseCore 0:
  24.3 56.5 reduce-scatter.4
  84.0 39.1 reduce-scatter.6
  126.4 81.6 all-gather.1
  226.1 63.1 all-reduce.1
